TPU v7x, 32 devices: a whole 2x2x4 slice. The times are simulated.
32 devices in a mesh: grp: 2 (over y), tile: 16 (over z, x, core).
Axes of the slice: x: 2, y: 2, z: 4, core: 2. Of those that a mesh axis runs over, the one named last changes fastest.
Arguments:
- rhs: float32 [256, 28672], P('grp', 'tile'), parts along dimension 0, may hold values from -4.5 to 4.5
- mass_diag: float32 [28672], P('tile'), may hold values from 0.1 to 2
- edge_heads: int32 [114688], P('tile'), may hold values from 128 to 1919
- edge_tails: int32 [114688], P('tile'), may hold values from 0 to 2047
- edge_weight: float32 [114688], P('tile'), may hold values from 0.5 to 2
- local_inverse: bfloat16 [32768, 2048], P('tile'), may hold values from -0.5 to 1
- coarse_vec: float32 [28672], P('tile'), may hold values from 0.25 to 1.75
- coarse_inv: float32 [16, 16], replicated, may hold values from -0.000558035714 to 0.002232143
Outputs:
- solution: float32 [256, 28672], P('grp', 'tile'), parts along dimension 0
- residual: float32 [256, 28672], P('grp', 'tile'), parts along dimension 0
There are 2 independent parts, one for each index of `grp`. A program takes and returns all parts, laid end to end along the dimension named above; an argument that names none is the same for every part. Nothing has to cross between parts.
All inputs are finite; a program needn't handle non-finite values.
Results may differ from a plain program's by a relative error of at most 0.015.
Values may be sent and summed in bfloat16 or wider, within the bound.
No kernel may reach another device: no remote copies, remote signals or barrier semaphores. Data moves between devices by JAX's collectives and lax.ppermute only.
A program may use at most 128 MiB of HBM per device.

v0:
```python
import jax
import jax.numpy as jnp
from jax import lax
from jax.sharding import PartitionSpec as P

SUB = 2048
STRIP = 128
ITERS = 2


def with_halo(block, sides, width):
    for axis, dim in sides:
        count = lax.axis_size(axis)
        forward = [(i, i + 1) for i in range(count - 1)]
        backward = [(target, source) for source, target in forward]
        low = lax.ppermute(
            lax.slice_in_dim(block, block.shape[dim] - width, None, axis=dim), axis, forward
        )
        high = lax.ppermute(lax.slice_in_dim(block, 0, width, axis=dim), axis, backward)
        block = jnp.concatenate([low, block, high], axis=dim)
    return block


def send_back(contrib):
    rims = jnp.concatenate([contrib[:, :STRIP], contrib[:, -STRIP:]], axis=1)
    arrived = with_halo(rims.astype(jnp.bfloat16), (("tile", 1),), STRIP).astype(rims.dtype)
    owned = contrib[:, STRIP:-STRIP]
    lower = owned[:, :STRIP] + arrived[:, :STRIP]
    upper = owned[:, -STRIP:] + arrived[:, -STRIP:]
    return jnp.concatenate([lower, owned[:, STRIP:-STRIP], upper], axis=1)


def build_stiffness(edge_heads, edge_tails, edge_weight):
    rows_idx = jnp.concatenate([edge_heads, edge_tails, edge_heads, edge_tails])
    cols_idx = jnp.concatenate([edge_heads, edge_tails, edge_tails, edge_heads])
    values = jnp.concatenate([edge_weight, edge_weight, -edge_weight, -edge_weight])
    return jnp.zeros((SUB, SUB), jnp.float32).at[rows_idx, cols_idx].add(values)


def operate(vector, mass_diag, stiffness):
    widened = with_halo(vector, (("tile", 1),), STRIP)
    contrib = jnp.dot(widened, stiffness, precision=lax.Precision.HIGHEST)
    return mass_diag * vector + send_back(contrib)


def precondition(resid, local_inverse, coarse_vec, coarse_inv):
    widened = with_halo(resid.astype(jnp.bfloat16), (("tile", 1),), STRIP)
    local = jnp.dot(widened, local_inverse, preferred_element_type=jnp.float32)
    schwarz = send_back(local)
    restricted = jnp.sum(resid * coarse_vec, axis=1)
    mine_index = lax.axis_index("tile")
    every = lax.all_gather(restricted[:, None], "tile", axis=1, tiled=True)
    column = lax.dynamic_slice_in_dim(coarse_inv, mine_index, 1, 1)
    mine = jnp.dot(every, column, precision=lax.Precision.HIGHEST)
    return schwarz + mine * coarse_vec


def inner(left, right):
    return jnp.sum(left * right, axis=1)


def both_dots(resid, zvec, image):
    return lax.psum((inner(resid, zvec), inner(image, zvec)), "tile")


def shards(
    rhs, mass_diag, edge_heads, edge_tails, edge_weight, local_inverse, coarse_vec, coarse_inv
):
    stiffness = build_stiffness(edge_heads, edge_tails, edge_weight)
    solution = jnp.zeros_like(rhs)
    resid = rhs
    zvec = precondition(resid, local_inverse, coarse_vec, coarse_inv)
    image = operate(zvec, mass_diag, stiffness)
    gamma, delta = both_dots(resid, zvec, image)
    alpha = gamma / delta
    direction, along = (zvec, image)
    for step in range(ITERS):
        solution = solution + alpha[:, None] * direction
        resid = resid - alpha[:, None] * along
        if step + 1 < ITERS:
            zvec = precondition(resid, local_inverse, coarse_vec, coarse_inv)
            image = operate(zvec, mass_diag, stiffness)
            gamma_next, delta = both_dots(resid, zvec, image)
            ratio = gamma_next / gamma
            alpha = gamma_next / (delta - ratio * gamma_next / alpha)
            direction = zvec + ratio[:, None] * direction
            along = image + ratio[:, None] * along
            gamma = gamma_next
    return (solution, resid)


def solution(mesh):
    return jax.shard_map(
        shards,
        mesh=mesh,
        in_specs=(
            P("grp", "tile"),
            P("tile"),
            P("tile"),
            P("tile"),
            P("tile"),
            P("tile", None),
            P("tile"),
            P(),
        ),
        out_specs=(P("grp", "tile"), P("grp", "tile")),
        check_vma=False,
    )
```

profile of v0, /device:TPU:0, one launch (start us, length us, event | category | flops | bytes accessed | tf_op | source)
XLA Modules:
  0.0 372.3 jit_solution(4083867110889075399)
XLA Ops:
  0.7 1.7 multiply_reduce_fusion.5
  2.4 1.3 collective-permute-start.1
  3.7 3.0 collective-permute-start
  6.7 1.1 compare_select_fusion.1
  7.8 0.5 and_reduce_fusion
  8.3 1.1 multiply_reduce_fusion.6
  9.4 0.2 dynamic-slice_reduce_fusion
  9.6 23.1 %all-gather = f32[16,1,128]{2,1,0:T(1,128)S(1)} all-gather(f32[1,1,128]{2,1,0:T(1,128)S(1)} %bitcast.29), channel_id=1, replica_groups=mesh['grp'=2,'tile'=16] {'tile'}, dimensions={0}, use_global_device_ids=true | all-gather | bytes 8704 | tf_op jit(solution)/shard_map/all_gather | solution.py:52
  32.7 4.7 %fusion.40 = (bf16[128,2048]{1,0:T(8,128)(2,1)S(1)}, f32[128,2048]{1,0:T(8,128)S(1)}) fusion(bf16[2048,2048]{1,0:T(8,128)(2,1)} %param.13, bf16[128,128]{1,0:T(8,128)(2,1)S(1)} %collective-permute-done.1, bf16[128,1792]{1,0:T(8,128)(2,1)S(1)} %get-tuple-element.29, bf16[128,128]{1,0:T(8,128)(2,1)S(1)} %collective-permute-done), kind=kOutput, calls=%fused_computation.86 | convolution fusion | flops 1075576832 | bytes 10485760 | tf_op jit(solution)/shard_map/dot_general | solution.py:48
  37.5 1.3 collective-permute-start.3
  38.8 3.0 collective-permute-start.2
  41.8 0.1 convolution_bitcast_fusion.1
  42.1 0.6 collective-permute-done.2
  42.7 0.1 maximum_add_fusion
  42.9 1.3 collective-permute-start.5
  44.2 4.3 %collective-permute-start.4 = (f32[128,128]{1,0:T(8,128)S(1)}, f32[128,128]{1,0:T(8,128)S(1)}, u32[]{:S(2)}, u32[]{:S(2)}) collective-permute-start(f32[128,128]{1,0:T(8,128)S(1)} %get-tuple-element.26), channel_id=1, source_target_pairs={{0,1},{1,2},{2,3},{3,4},{4,5},{5,6},{6,7},{7,8},{8,9},{9,10},{10,1... | collective-permute-start | bytes 196616 | tf_op jit(solution)/shard_map/ppermute | solution.py:16
  48.5 156.5 %scatter_custom_fusion = f32[4194304]{0:T(1024)} fusion(s32[28672]{0:T(1024)S(1)} %broadcast_select_fusion, f32[28672]{0:T(1024)S(1)} %pad_maximum_fusion, f32[]{:T(128)} %constant.5.clone.1), kind=kCustom, calls=%fused_computation.1 | custom fusion | flops 28672 | bytes 16777220
  205.0 18.0 %reshape.335 = f32[2048,2048]{1,0:T(8,128)} reshape(f32[4194304]{0:T(1024)} %scatter_custom_fusion) | data formatting | bytes 33554432 | tf_op jit(solution)/shard_map/scatter-add | solution.py:37
  223.0 12.8 %fusion.41 = (bf16[128,2048]{1,0:T(8,128)(2,1)S(1)}, f32[128,2048]{1,0:T(8,128)S(1)}) fusion(f32[2048,2048]{1,0:T(8,128)} %reshape.335, f32[128,128]{1,0:T(8,128)S(1)} %collective-permute-done.5, f32[128,1792]{1,0:T(8,128)S(1)} %maximum_add_fusion, f32[128,128]{1,0:T(8,128)S(1)} %collective-permute-done.4), kind=kOutput, calls=%fused_computation.87 | convolution fusion | flops 6443237376 | bytes 19398656 | tf_op jit(solution)/shard_map/dot_general | solution.py:42
  235.8 1.3 collective-permute-start.7
  237.1 5.0 %collective-permute-start.6 = (bf16[128,128]{1,0:T(8,128)(2,1)S(1)}, bf16[128,128]{1,0:T(8,128)(2,1)S(1)}, u32[]{:S(2)}, u32[]{:S(2)}) collective-permute-start(bf16[128,128]{1,0:T(8,128)(2,1)S(1)} %get-tuple-element.34), channel_id=1, source_target_pairs={{0,1},{1,2},{2,3},{3,4},{4,5},{5,6},{6,7},{7,8},{8,9},{9,10},{10,1... | collective-permute-start | bytes 98312 | tf_op jit(solution)/shard_map/ppermute | solution.py:16
  242.2 0.6 collective-permute-done.6
  242.9 0.3 multiply_reduce_fusion.3
  243.2 31.4 %all-reduce.1 = (f32[128]{0:T(128)S(1)}, f32[128]{0:T(128)S(1)}) all-reduce(f32[128]{0:T(128)S(1)} %get-tuple-element.5, f32[128]{0:T(128)S(1)} %get-tuple-element.4), channel_id=1, replica_groups=mesh['grp'=2,'tile'=16] {'tile'}, use_global_device_ids=true, to_apply=%region_2.0 | all-reduce | flops 256 | bytes 2048 | tf_op jit(solution)/shard_map/psum | solution.py:63
  274.6 0.5 copy-done.13
  275.1 1.2 multiply_reduce_fusion.2
  276.4 1.3 collective-permute-start.9
  277.7 3.0 collective-permute-start.8
  280.7 17.1 %all-gather.1 = f32[16,1,128]{2,1,0:T(1,128)S(1)} all-gather(f32[1,1,128]{2,1,0:T(1,128)S(1)} %bitcast.30), channel_id=1, replica_groups=mesh['grp'=2,'tile'=16] {'tile'}, dimensions={0}, use_global_device_ids=true | all-gather | bytes 8704 | tf_op jit(solution)/shard_map/all_gather | solution.py:52
  297.9 4.7 %fusion.42 = (bf16[128,2048]{1,0:T(8,128)(2,1)S(1)}, f32[128,2048]{1,0:T(8,128)S(1)}) fusion(bf16[2048,2048]{1,0:T(8,128)(2,1)} %param.13, bf16[128,128]{1,0:T(8,128)(2,1)S(1)} %collective-permute-done.9, bf16[128,1792]{1,0:T(8,128)(2,1)S(1)} %convert_element_type.25, bf16[128,128]{1,0:T(8,128)(2,1)S(1)} %collective-permute-done.8), kind=kOutput, calls=%fused_computation.88 | convolution fusion | flops 1075576832 | bytes 10485760 | tf_op jit(solution)/shard_map/dot_general | solution.py:48
  302.6 1.3 collective-permute-start.11
  303.9 3.0 collective-permute-start.10
  306.9 0.8 convolution_bitcast_fusion
  307.7 0.1 slice.195
  307.8 0.1 maximum_add_fusion.2
  308.0 1.3 collective-permute-start.13
  309.3 4.3 %collective-permute-start.12 = (f32[128,128]{1,0:T(8,128)S(1)}, f32[128,128]{1,0:T(8,128)S(1)}, u32[]{:S(2)}, u32[]{:S(2)}) collective-permute-start(f32[128,128]{1,0:T(8,128)S(1)} %get-tuple-element.24), channel_id=1, source_target_pairs={{0,1},{1,2},{2,3},{3,4},{4,5},{5,6},{6,7},{7,8},{8,9},{9,10},{10,1... | collective-permute-start | bytes 196616 | tf_op jit(solution)/shard_map/ppermute | solution.py:16
  313.6 0.9 collective-permute-done.12
  314.5 12.7 %fusion.43 = (bf16[128,2048]{1,0:T(8,128)(2,1)S(1)}, f32[128,2048]{1,0:T(8,128)S(1)}) fusion(f32[2048,2048]{1,0:T(8,128)} %reshape.335, f32[128,128]{1,0:T(8,128)S(1)} %collective-permute-done.13, f32[128,1792]{1,0:T(8,128)S(1)} %maximum_add_fusion.2, f32[128,128]{1,0:T(8,128)S(1)} %collective-permute-done.12), kind=kOutput, calls=%fused_computation.89 | convolution fusion | flops 6443237376 | bytes 19398656 | tf_op jit(solution)/shard_map/dot_general | solution.py:42
  327.2 1.3 collective-permute-start.15
  328.5 5.9 %collective-permute-start.14 = (bf16[128,128]{1,0:T(8,128)(2,1)S(1)}, bf16[128,128]{1,0:T(8,128)(2,1)S(1)}, u32[]{:S(2)}, u32[]{:S(2)}) collective-permute-start(bf16[128,128]{1,0:T(8,128)(2,1)S(1)} %get-tuple-element.30), channel_id=1, source_target_pairs={{0,1},{1,2},{2,3},{3,4},{4,5},{5,6},{6,7},{7,8},{8,9},{9,10},{10,1... | collective-permute-start | bytes 98312 | tf_op jit(solution)/shard_map/ppermute | solution.py:16
  334.5 0.8 collective-permute-done.14
  335.3 0.1 copy-done.2
  335.3 0.3 multiply_reduce_fusion
  335.6 0.2 copy-done.5
  335.9 32.6 %all-reduce = (f32[128]{0:T(128)}, f32[128]{0:T(128)}) all-reduce(f32[128]{0:T(128)S(1)} %get-tuple-element.3, f32[128]{0:T(128)S(1)} %get-tuple-element.2), channel_id=1, replica_groups=mesh['grp'=2,'tile'=16] {'tile'}, use_global_device_ids=true, to_apply=%region_8.0 | all-reduce | flops 256 | bytes 2048 | tf_op jit(solution)/shard_map/psum | solution.py:63
  368.5 0.7 subtract_divide_fusion
  369.2 3.1 multiply_subtract_fusion
  (59 shorter events, 0.5 us)
Async XLA Ops:
  0.6 8.8 %copy-start = (f32[16,16]{1,0:T(8,128)S(1)}, f32[16,16]{1,0:T(8,128)}, u32[]{:S(2)}) copy-start(f32[16,16]{1,0:T(8,128)} %param.15) | copy-start | bytes 3076
  0.6 42.1 %copy-start.7 = (f32[1792]{0:T(1024)S(1)}, f32[1792]{0:T(1024)}, u32[]{:S(2)}) copy-start(f32[1792]{0:T(1024)} %param.14) | copy-start | bytes 21508
  0.7 41.3 %copy-start.10 = (f32[7168]{0:T(1024)S(1)}, f32[7168]{0:T(1024)}, u32[]{:S(2)}) copy-start(f32[7168]{0:T(1024)} %param.12) | copy-start | bytes 86020
  2.4 30.4 %collective-permute-start.1 = (bf16[128,128]{1,0:T(8,128)(2,1)S(1)}, bf16[128,128]{1,0:T(8,128)(2,1)S(1)}, u32[]{:S(2)}, u32[]{:S(2)}) collective-permute-start(bf16[128,128]{1,0:T(8,128)(2,1)S(1)} %get-tuple-element.41), channel_id=1, source_target_pairs={{1,0},{2,1},{3,2},{4,3},{5,4},{6,5},{7,6},{8,7},{9,8},{10,9},{11,1... | collective-permute-start | bytes 98312 | tf_op jit(solution)/shard_map/ppermute | solution.py:19
  3.7 29.1 %collective-permute-start = (bf16[128,128]{1,0:T(8,128)(2,1)S(1)}, bf16[128,128]{1,0:T(8,128)(2,1)S(1)}, u32[]{:S(2)}, u32[]{:S(2)}) collective-permute-start(bf16[128,128]{1,0:T(8,128)(2,1)S(1)} %get-tuple-element.40), channel_id=1, source_target_pairs={{0,1},{1,2},{2,3},{3,4},{4,5},{5,6},{6,7},{7,8},{8,9},{9,10},{10,1... | collective-permute-start | bytes 98312 | tf_op jit(solution)/shard_map/ppermute | solution.py:16
  9.6 33.1 %copy-start.11 = (f32[16]{0:T(128)}, f32[16]{0:T(128)S(1)}, u32[]{:S(2)}) copy-start(f32[16]{0:T(128)S(1)} %dynamic-slice_reduce_fusion) | copy-start | bytes 196
  37.5 4.6 %collective-permute-start.3 = (bf16[128,128]{1,0:T(8,128)(2,1)S(1)}, bf16[128,128]{1,0:T(8,128)(2,1)S(1)}, u32[]{:S(2)}, u32[]{:S(2)}) collective-permute-start(bf16[128,128]{1,0:T(8,128)(2,1)S(1)} %get-tuple-element.37), channel_id=1, source_target_pairs={{1,0},{2,1},{3,2},{4,3},{5,4},{6,5},{7,6},{8,7},{9,8},{10,9},{11,1... | collective-permute-start | bytes 98312 | tf_op jit(solution)/shard_map/ppermute | solution.py:19
  38.8 3.9 %collective-permute-start.2 = (bf16[128,128]{1,0:T(8,128)(2,1)S(1)}, bf16[128,128]{1,0:T(8,128)(2,1)S(1)}, u32[]{:S(2)}, u32[]{:S(2)}) collective-permute-start(bf16[128,128]{1,0:T(8,128)(2,1)S(1)} %get-tuple-element.36), channel_id=1, source_target_pairs={{0,1},{1,2},{2,3},{3,4},{4,5},{5,6},{6,7},{7,8},{8,9},{9,10},{10,1... | collective-permute-start | bytes 98312 | tf_op jit(solution)/shard_map/ppermute | solution.py:16
  42.9 180.1 %collective-permute-start.5 = (f32[128,128]{1,0:T(8,128)S(1)}, f32[128,128]{1,0:T(8,128)S(1)}, u32[]{:S(2)}, u32[]{:S(2)}) collective-permute-start(f32[128,128]{1,0:T(8,128)S(1)} %get-tuple-element.27), channel_id=1, source_target_pairs={{1,0},{2,1},{3,2},{4,3},{5,4},{6,5},{7,6},{8,7},{9,8},{10,9},{11,1... | collective-permute-start | bytes 196616 | tf_op jit(solution)/shard_map/ppermute | solution.py:19
  44.2 178.8 %collective-permute-start.4 = (f32[128,128]{1,0:T(8,128)S(1)}, f32[128,128]{1,0:T(8,128)S(1)}, u32[]{:S(2)}, u32[]{:S(2)}) collective-permute-start(f32[128,128]{1,0:T(8,128)S(1)} %get-tuple-element.26), channel_id=1, source_target_pairs={{0,1},{1,2},{2,3},{3,4},{4,5},{5,6},{6,7},{7,8},{8,9},{9,10},{10,1... | collective-permute-start | bytes 196616 | tf_op jit(solution)/shard_map/ppermute | solution.py:16
  223.0 19.9 %copy-start.1 = (f32[128,1792]{1,0:T(8,128)S(1)}, f32[128,1792]{1,0:T(8,128)}, u32[]{:S(2)}) copy-start(f32[128,1792]{1,0:T(8,128)} %param.8) | copy-start | bytes 2752516
  223.0 19.9 %copy-start.8 = (f32[1792]{0:T(1024)S(1)}, f32[1792]{0:T(1024)}, u32[]{:S(2)}) copy-start(f32[1792]{0:T(1024)} %param.9) | copy-start | bytes 21508
  235.8 6.4 %collective-permute-start.7 = (bf16[128,128]{1,0:T(8,128)(2,1)S(1)}, bf16[128,128]{1,0:T(8,128)(2,1)S(1)}, u32[]{:S(2)}, u32[]{:S(2)}) collective-permute-start(bf16[128,128]{1,0:T(8,128)(2,1)S(1)} %get-tuple-element.35), channel_id=1, source_target_pairs={{1,0},{2,1},{3,2},{4,3},{5,4},{6,5},{7,6},{8,7},{9,8},{10,9},{11,1... | collective-permute-start | bytes 98312 | tf_op jit(solution)/shard_map/ppermute | solution.py:19
  237.1 5.7 %collective-permute-start.6 = (bf16[128,128]{1,0:T(8,128)(2,1)S(1)}, bf16[128,128]{1,0:T(8,128)(2,1)S(1)}, u32[]{:S(2)}, u32[]{:S(2)}) collective-permute-start(bf16[128,128]{1,0:T(8,128)(2,1)S(1)} %get-tuple-element.34), channel_id=1, source_target_pairs={{0,1},{1,2},{2,3},{3,4},{4,5},{5,6},{6,7},{7,8},{8,9},{9,10},{10,1... | collective-permute-start | bytes 98312 | tf_op jit(solution)/shard_map/ppermute | solution.py:16
  242.8 31.7 %copy-start.3 = (f32[128,128]{1,0:T(8,128)}, f32[128,128]{1,0:T(8,128)S(1)}, u32[]{:S(2)}) copy-start(f32[128,128]{1,0:T(8,128)S(1)} %get-tuple-element.20) | copy-start | bytes 196612
  242.8 31.7 %copy-start.4 = (f32[128,128]{1,0:T(8,128)}, f32[128,128]{1,0:T(8,128)S(1)}, u32[]{:S(2)}) copy-start(f32[128,128]{1,0:T(8,128)S(1)} %get-tuple-element.21) | copy-start | bytes 196612
  274.5 0.5 copy-start.13
  274.5 0.5 copy-start.14
  275.1 22.8 %copy-start.12 = (f32[128]{0:T(128)}, f32[128]{0:T(128)S(1)}, u32[]{:S(2)}) copy-start(f32[128]{0:T(128)S(1)} %div.12) | copy-start | bytes 1540
  276.4 21.5 %collective-permute-start.9 = (bf16[128,128]{1,0:T(8,128)(2,1)S(1)}, bf16[128,128]{1,0:T(8,128)(2,1)S(1)}, u32[]{:S(2)}, u32[]{:S(2)}) collective-permute-start(bf16[128,128]{1,0:T(8,128)(2,1)S(1)} %get-tuple-element.39), channel_id=1, source_target_pairs={{1,0},{2,1},{3,2},{4,3},{5,4},{6,5},{7,6},{8,7},{9,8},{10,9},{11,1... | collective-permute-start | bytes 98312 | tf_op jit(solution)/shard_map/ppermute | solution.py:19
  277.7 20.2 %collective-permute-start.8 = (bf16[128,128]{1,0:T(8,128)(2,1)S(1)}, bf16[128,128]{1,0:T(8,128)(2,1)S(1)}, u32[]{:S(2)}, u32[]{:S(2)}) collective-permute-start(bf16[128,128]{1,0:T(8,128)(2,1)S(1)} %get-tuple-element.38), channel_id=1, source_target_pairs={{0,1},{1,2},{2,3},{3,4},{4,5},{5,6},{6,7},{7,8},{8,9},{9,10},{10,1... | collective-permute-start | bytes 98312 | tf_op jit(solution)/shard_map/ppermute | solution.py:16
  302.6 32.8 %copy-start.9 = (f32[1792]{0:T(1024)S(1)}, f32[1792]{0:T(1024)}, u32[]{:S(2)}) copy-start(f32[1792]{0:T(1024)} %param.9) | copy-start | bytes 21508
  302.6 5.2 %collective-permute-start.11 = (bf16[128,128]{1,0:T(8,128)(2,1)S(1)}, bf16[128,128]{1,0:T(8,128)(2,1)S(1)}, u32[]{:S(2)}, u32[]{:S(2)}) collective-permute-start(bf16[128,128]{1,0:T(8,128)(2,1)S(1)} %get-tuple-element.33), channel_id=1, source_target_pairs={{1,0},{2,1},{3,2},{4,3},{5,4},{6,5},{7,6},{8,7},{9,8},{10,9},{11,1... | collective-permute-start | bytes 98312 | tf_op jit(solution)/shard_map/ppermute | solution.py:19
  303.9 3.9 %collective-permute-start.10 = (bf16[128,128]{1,0:T(8,128)(2,1)S(1)}, bf16[128,128]{1,0:T(8,128)(2,1)S(1)}, u32[]{:S(2)}, u32[]{:S(2)}) collective-permute-start(bf16[128,128]{1,0:T(8,128)(2,1)S(1)} %get-tuple-element.32), channel_id=1, source_target_pairs={{0,1},{1,2},{2,3},{3,4},{4,5},{5,6},{6,7},{7,8},{8,9},{9,10},{10,1... | collective-permute-start | bytes 98312 | tf_op jit(solution)/shard_map/ppermute | solution.py:16
  308.0 5.6 %collective-permute-start.13 = (f32[128,128]{1,0:T(8,128)S(1)}, f32[128,128]{1,0:T(8,128)S(1)}, u32[]{:S(2)}, u32[]{:S(2)}) collective-permute-start(f32[128,128]{1,0:T(8,128)S(1)} %get-tuple-element.25), channel_id=1, source_target_pairs={{1,0},{2,1},{3,2},{4,3},{5,4},{6,5},{7,6},{8,7},{9,8},{10,9},{11,1... | collective-permute-start | bytes 196616 | tf_op jit(solution)/shard_map/ppermute | solution.py:19
  309.3 5.2 %collective-permute-start.12 = (f32[128,128]{1,0:T(8,128)S(1)}, f32[128,128]{1,0:T(8,128)S(1)}, u32[]{:S(2)}, u32[]{:S(2)}) collective-permute-start(f32[128,128]{1,0:T(8,128)S(1)} %get-tuple-element.24), channel_id=1, source_target_pairs={{0,1},{1,2},{2,3},{3,4},{4,5},{5,6},{6,7},{7,8},{8,9},{9,10},{10,1... | collective-permute-start | bytes 196616 | tf_op jit(solution)/shard_map/ppermute | solution.py:16
  327.2 7.2 %collective-permute-start.15 = (bf16[128,128]{1,0:T(8,128)(2,1)S(1)}, bf16[128,128]{1,0:T(8,128)(2,1)S(1)}, u32[]{:S(2)}, u32[]{:S(2)}) collective-permute-start(bf16[128,128]{1,0:T(8,128)(2,1)S(1)} %get-tuple-element.31), channel_id=1, source_target_pairs={{1,0},{2,1},{3,2},{4,3},{5,4},{6,5},{7,6},{8,7},{9,8},{10,9},{11,1... | collective-permute-start | bytes 98312 | tf_op jit(solution)/shard_map/ppermute | solution.py:19
  328.5 6.7 %collective-permute-start.14 = (bf16[128,128]{1,0:T(8,128)(2,1)S(1)}, bf16[128,128]{1,0:T(8,128)(2,1)S(1)}, u32[]{:S(2)}, u32[]{:S(2)}) collective-permute-start(bf16[128,128]{1,0:T(8,128)(2,1)S(1)} %get-tuple-element.30), channel_id=1, source_target_pairs={{0,1},{1,2},{2,3},{3,4},{4,5},{5,6},{6,7},{7,8},{8,9},{9,10},{10,1... | collective-permute-start | bytes 98312 | tf_op jit(solution)/shard_map/ppermute | solution.py:16
  334.4 0.9 copy-start.2
  335.2 0.6 copy-start.5
  335.2 0.7 copy-start.6
where the time goes:
time: 374 us; the launch traced here: 372 us
  other arithmetic  167 us (45%)
  blocking collectives  104 us (28%)
  starting transfers between devices  41.9 us (11%)
  matrix products  35.9 us (10%)
  local copies, waits for them, and re-layouts  19.4 us (5%)
    unnamed x4, other arithmetic  158 us
    psum x2, blocking collectives, both_dots(): return lax.psum((inner(resid, zvec), inner(image, zvec)), 'tile')  64 us
    all_gather x2, blocking collectives, precondition(): every = lax.all_gather(restricted[:, None], 'tile', axis=1, tiled=True)  40.3 us
    ppermute x8, starting transfers between devices, with_halo(): lax.ppermute(lax.slice_in_dim(block, block.shape[dim] - width, None, axis...  31.6 us
    dot_general x2, matrix products, operate(): contrib = jnp.dot(widened, stiffness, precision=lax.Precision.HIGHEST)  25.5 us
    scatter-add x1, local copies, waits for them, and re-layouts, build_stiffness(): return jnp.zeros((SUB, SUB), jnp.float32).at[rows_idx, cols_idx].add(values)  18 us
    ppermute x8, starting transfers between devices, with_halo(): lax.ppermute(lax.slice_in_dim(block, 0, width, axis=dim), axis, backward)  10.3 us
    dot_general x2, matrix products, precondition(): local = jnp.dot(widened, local_inverse, preferred_element_type=jnp.float32)  9.43 us
  transfers between devices with their start and end apart: 16, of which 4 were waited for; matrix products, arithmetic and copies ran while one was open for 48% of the time, Pallas kernels for 0%

commit v1 on v0

--- a/solution.py
+++ b/solution.py
@@ -49,7 +49,21 @@
     schwarz = send_back(local)
     restricted = jnp.sum(resid * coarse_vec, axis=1)
     mine_index = lax.axis_index("tile")
-    every = lax.all_gather(restricted[:, None], "tile", axis=1, tiled=True)
+    array = restricted[:, None]
+    ways, here, k = (lax.axis_size("tile"), lax.axis_index("tile"), array.shape[1])
+    shape = [n * ways if d == 1 else n for d, n in enumerate(array.shape)]
+    every = lax.dynamic_update_slice_in_dim(jnp.zeros(shape, array.dtype), array, here * k, axis=1)
+    going_up = going_down = array
+    for far in range(1, ways // 2 + 1):
+        going_up = lax.ppermute(going_up, "tile", [(d, (d + 1) % ways) for d in range(ways)])
+        every = lax.dynamic_update_slice_in_dim(every, going_up, (here - far) % ways * k, axis=1)
+        if 2 * far < ways:
+            going_down = lax.ppermute(
+                going_down, "tile", [(d, (d - 1) % ways) for d in range(ways)]
+            )
+            every = lax.dynamic_update_slice_in_dim(
+                every, going_down, (here + far) % ways * k, axis=1
+            )
     column = lax.dynamic_slice_in_dim(coarse_inv, mine_index, 1, 1)
     mine = jnp.dot(every, column, precision=lax.Precision.HIGHEST)
     return schwarz + mine * coarse_vec

time: 374 us -> 421 us (1.13)
  starting transfers between devices: 41.9 us -> 101 us
  blocking collectives: 104 us -> 63.9 us
  waiting for transfers between devices: 2.86 us -> 28.1 us
    ppermute x0 -> x30, starting transfers between devices: none -> 63 us  [the longest x14 62.3 us: precondition(): lax.ppermute(going_down, 'tile', [(d, (d - 1) % ways) for d in range(ways)])]
    all_gather x2 -> x0, blocking collectives: 40.3 us -> none  [precondition(): every = lax.all_gather(restricted[:, None], 'tile', axis=1, tiled=True)]
    ppermute x0 -> x30, waiting for transfers between devices: none -> 25.3 us  [the longest x16 21.8 us: precondition(): lax.ppermute(going_up, 'tile', [(d, (d + 1) % ways) for d in range(ways)])]
  transfers between devices with their start and end apart: 16 -> 46, of which waited for: 4 -> 24; matrix products, arithmetic and copies ran while one was open for 48% -> 43% of each run, Pallas kernels for 0% -> 0%
where the time goes in v1:
time: 421 us; the launch traced here: 419 us
  other arithmetic  168 us (40%)
  starting transfers between devices  101 us (24%)
  blocking collectives  63.9 us (15%)
  matrix products  35.9 us (9%)
  waiting for transfers between devices  28.1 us (7%)
  local copies, waits for them, and re-layouts  21.2 us (5%)
    unnamed x4, other arithmetic  158 us
    psum x2, blocking collectives, both_dots(): return lax.psum((inner(resid, zvec), inner(image, zvec)), 'tile')  63.9 us
    ppermute x14, starting transfers between devices, precondition(): lax.ppermute(going_down, 'tile', [(d, (d - 1) % ways) for d in range(ways)])  62.3 us
    ppermute x8, starting transfers between devices, with_halo(): lax.ppermute(lax.slice_in_dim(block, block.shape[dim] - width, None, axis...  27.9 us
    dot_general x2, matrix products, operate(): contrib = jnp.dot(widened, stiffness, precision=lax.Precision.HIGHEST)  25.5 us
    ppermute x16, waiting for transfers between devices, precondition(): lax.ppermute(going_up, 'tile', [(d, (d + 1) % ways) for d in range(ways)])  21.8 us
    scatter-add x1, local copies, waits for them, and re-layouts, build_stiffness(): return jnp.zeros((SUB, SUB), jnp.float32).at[rows_idx, cols_idx].add(values)  18 us
    ppermute x8, starting transfers between devices, with_halo(): lax.ppermute(lax.slice_in_dim(block, 0, width, axis=dim), axis, backward)  10.3 us
  transfers between devices with their start and end apart: 46, of which 24 were waited for; matrix products, arithmetic and copies ran while one was open for 43% of the time, Pallas kernels for 0%

profile of v1, /device:TPU:0, one launch (start us, length us, event | category | flops | bytes accessed | tf_op | source)
XLA Modules:
  0.0 419.4 jit_solution(9729947994448643924)
XLA Ops:
  0.7 1.7 multiply_reduce_fusion.5
  2.9 5.0 %collective-permute-start.5 = (f32[128,1]{0,1:T(1,128)S(1)}, f32[128,1]{0,1:T(1,128)S(1)}, u32[]{:S(2)}, u32[]{:S(2)}) collective-permute-start(f32[128,1]{0,1:T(1,128)S(1)} %bitcast.22), channel_id=1, source_target_pairs={{0,15},{1,0},{2,1},{3,2},{4,3},{5,4},{6,5},{7,6},{8,7},{9,8},{10,9... | collective-permute-start | bytes 1544 | tf_op jit(solution)/shard_map/ppermute | solution.py:61
  7.9 1.3 collective-permute-start.1
  9.2 3.0 collective-permute-start
  15.3 4.4 %collective-permute-start.7 = (f32[128,1]{0,1:T(1,128)S(1)}, f32[128,1]{0,1:T(1,128)S(1)}, u32[]{:S(2)}, u32[]{:S(2)}) collective-permute-start(f32[128,1]{0,1:T(1,128)S(1)} %collective-permute-done.5), channel_id=1, source_target_pairs={{0,15},{1,0},{2,1},{3,2},{4,3},{5,4},{6,5},{7,6},{8,7},{9,8},{10,9... | collective-permute-start | bytes 1544 | tf_op jit(solution)/shard_map/ppermute | solution.py:61
  19.7 1.2 collective-permute-done.6
  21.0 4.4 %collective-permute-start.9 = (f32[128,1]{0,1:T(1,128)S(1)}, f32[128,1]{0,1:T(1,128)S(1)}, u32[]{:S(2)}, u32[]{:S(2)}) collective-permute-start(f32[128,1]{0,1:T(1,128)S(1)} %collective-permute-done.7), channel_id=1, source_target_pairs={{0,15},{1,0},{2,1},{3,2},{4,3},{5,4},{6,5},{7,6},{8,7},{9,8},{10,9... | collective-permute-start | bytes 1544 | tf_op jit(solution)/shard_map/ppermute | solution.py:61
  25.4 1.2 collective-permute-done.8
  27.4 4.4 %collective-permute-start.11 = (f32[128,1]{0,1:T(1,128)S(1)}, f32[128,1]{0,1:T(1,128)S(1)}, u32[]{:S(2)}, u32[]{:S(2)}) collective-permute-start(f32[128,1]{0,1:T(1,128)S(1)} %collective-permute-done.9), channel_id=1, source_target_pairs={{0,15},{1,0},{2,1},{3,2},{4,3},{5,4},{6,5},{7,6},{8,7},{9,8},{10,9... | collective-permute-start | bytes 1544 | tf_op jit(solution)/shard_map/ppermute | solution.py:61
  33.1 4.4 %collective-permute-start.13 = (f32[128,1]{0,1:T(1,128)S(1)}, f32[128,1]{0,1:T(1,128)S(1)}, u32[]{:S(2)}, u32[]{:S(2)}) collective-permute-start(f32[128,1]{0,1:T(1,128)S(1)} %collective-permute-done.11), channel_id=1, source_target_pairs={{0,15},{1,0},{2,1},{3,2},{4,3},{5,4},{6,5},{7,6},{8,7},{9,8},{10,9... | collective-permute-start | bytes 1544 | tf_op jit(solution)/shard_map/ppermute | solution.py:61
  38.8 4.4 %collective-permute-start.15 = (f32[128,1]{0,1:T(1,128)S(1)}, f32[128,1]{0,1:T(1,128)S(1)}, u32[]{:S(2)}, u32[]{:S(2)}) collective-permute-start(f32[128,1]{0,1:T(1,128)S(1)} %collective-permute-done.13), channel_id=1, source_target_pairs={{0,15},{1,0},{2,1},{3,2},{4,3},{5,4},{6,5},{7,6},{8,7},{9,8},{10,9... | collective-permute-start | bytes 1544 | tf_op jit(solution)/shard_map/ppermute | solution.py:61
  44.5 4.4 %collective-permute-start.17 = (f32[128,1]{0,1:T(1,128)S(1)}, f32[128,1]{0,1:T(1,128)S(1)}, u32[]{:S(2)}, u32[]{:S(2)}) collective-permute-start(f32[128,1]{0,1:T(1,128)S(1)} %collective-permute-done.15), channel_id=1, source_target_pairs={{0,15},{1,0},{2,1},{3,2},{4,3},{5,4},{6,5},{7,6},{8,7},{9,8},{10,9... | collective-permute-start | bytes 1544 | tf_op jit(solution)/shard_map/ppermute | solution.py:61
  50.2 4.9 %collective-permute-done.18 = f32[128,1]{0,1:T(1,128)S(1)} collective-permute-done((f32[128,1]{0,1:T(1,128)S(1)}, f32[128,1]{0,1:T(1,128)S(1)}, u32[]{:S(2)}, u32[]{:S(2)}) %collective-permute-start.18) | collective-permute-done | bytes 544 | tf_op jit(solution)/shard_map/ppermute | solution.py:58
  55.1 4.7 %fusion.40 = (bf16[128,2048]{1,0:T(8,128)(2,1)S(1)}, f32[128,2048]{1,0:T(8,128)S(1)}) fusion(bf16[2048,2048]{1,0:T(8,128)(2,1)} %param.13, bf16[128,128]{1,0:T(8,128)(2,1)S(1)} %collective-permute-done.1, bf16[128,1792]{1,0:T(8,128)(2,1)S(1)} %get-tuple-element.29, bf16[128,128]{1,0:T(8,128)(2,1)S(1)} %collective-permute-done), kind=kOutput, calls=%fused_computation.86 | convolution fusion | flops 1075576832 | bytes 10485760 | tf_op jit(solution)/shard_map/dot_general | solution.py:48
  59.9 1.3 collective-permute-start.3
  61.2 3.0 collective-permute-start.2
  65.2 1.3 collective-permute-start.20
  66.5 3.0 collective-permute-start.19
  69.6 156.5 %scatter_custom_fusion = f32[4194304]{0:T(1024)} fusion(s32[28672]{0:T(1024)S(1)} %broadcast_select_fusion, f32[28672]{0:T(1024)S(1)} %pad_maximum_fusion, f32[]{:T(128)} %constant.121.clone.1), kind=kCustom, calls=%fused_computation.1 | custom fusion | flops 28672 | bytes 16777220
  226.1 18.0 %reshape.335 = f32[2048,2048]{1,0:T(8,128)} reshape(f32[4194304]{0:T(1024)} %scatter_custom_fusion) | data formatting | bytes 33554432 | tf_op jit(solution)/shard_map/scatter-add | solution.py:37
  244.1 12.8 %fusion.41 = (bf16[128,2048]{1,0:T(8,128)(2,1)S(1)}, f32[128,2048]{1,0:T(8,128)S(1)}) fusion(f32[2048,2048]{1,0:T(8,128)} %reshape.335, f32[128,128]{1,0:T(8,128)S(1)} %collective-permute-done.20, f32[128,1792]{1,0:T(8,128)S(1)} %maximum_add_fusion, f32[128,128]{1,0:T(8,128)S(1)} %collective-permute-done.19), kind=kOutput, calls=%fused_computation.87 | convolution fusion | flops 6443237376 | bytes 19398656 | tf_op jit(solution)/shard_map/dot_general | solution.py:42
  257.0 1.3 collective-permute-start.22
  258.3 4.5 %collective-permute-start.21 = (bf16[128,128]{1,0:T(8,128)(2,1)S(1)}, bf16[128,128]{1,0:T(8,128)(2,1)S(1)}, u32[]{:S(2)}, u32[]{:S(2)}) collective-permute-start(bf16[128,128]{1,0:T(8,128)(2,1)S(1)} %get-tuple-element.34), channel_id=1, source_target_pairs={{0,1},{1,2},{2,3},{3,4},{4,5},{5,6},{6,7},{7,8},{8,9},{9,10},{10,1... | collective-permute-start | bytes 98312 | tf_op jit(solution)/shard_map/ppermute | solution.py:16
  264.0 31.4 %all-reduce.1 = (f32[128]{0:T(128)S(1)}, f32[128]{0:T(128)S(1)}) all-reduce(f32[128]{0:T(128)S(1)} %get-tuple-element.5, f32[128]{0:T(128)S(1)} %get-tuple-element.4), channel_id=1, replica_groups=mesh['grp'=2,'tile'=16] {'tile'}, use_global_device_ids=true, to_apply=%region_2.3 | all-reduce | flops 256 | bytes 2048 | tf_op jit(solution)/shard_map/psum | solution.py:77
  297.3 1.3 collective-permute-start.24
  298.6 3.0 collective-permute-start.23
  301.7 4.4 %collective-permute-start.28 = (f32[128,1]{0,1:T(1,128)S(1)}, f32[128,1]{0,1:T(1,128)S(1)}, u32[]{:S(2)}, u32[]{:S(2)}) collective-permute-start(f32[128,1]{0,1:T(1,128)S(1)} %bitcast.25), channel_id=1, source_target_pairs={{0,15},{1,0},{2,1},{3,2},{4,3},{5,4},{6,5},{7,6},{8,7},{9,8},{10,9... | collective-permute-start | bytes 1544 | tf_op jit(solution)/shard_map/ppermute | solution.py:61
  306.1 1.2 collective-permute-done.27
  307.4 4.4 %collective-permute-start.30 = (f32[128,1]{0,1:T(1,128)S(1)}, f32[128,1]{0,1:T(1,128)S(1)}, u32[]{:S(2)}, u32[]{:S(2)}) collective-permute-start(f32[128,1]{0,1:T(1,128)S(1)} %collective-permute-done.28), channel_id=1, source_target_pairs={{0,15},{1,0},{2,1},{3,2},{4,3},{5,4},{6,5},{7,6},{8,7},{9,8},{10,9... | collective-permute-start | bytes 1544 | tf_op jit(solution)/shard_map/ppermute | solution.py:61
  311.8 1.2 collective-permute-done.29
  313.1 4.4 %collective-permute-start.32 = (f32[128,1]{0,1:T(1,128)S(1)}, f32[128,1]{0,1:T(1,128)S(1)}, u32[]{:S(2)}, u32[]{:S(2)}) collective-permute-start(f32[128,1]{0,1:T(1,128)S(1)} %collective-permute-done.30), channel_id=1, source_target_pairs={{0,15},{1,0},{2,1},{3,2},{4,3},{5,4},{6,5},{7,6},{8,7},{9,8},{10,9... | collective-permute-start | bytes 1544 | tf_op jit(solution)/shard_map/ppermute | solution.py:61
  317.5 1.2 collective-permute-done.31
  318.8 4.4 %collective-permute-start.34 = (f32[128,1]{0,1:T(1,128)S(1)}, f32[128,1]{0,1:T(1,128)S(1)}, u32[]{:S(2)}, u32[]{:S(2)}) collective-permute-start(f32[128,1]{0,1:T(1,128)S(1)} %collective-permute-done.32), channel_id=1, source_target_pairs={{0,15},{1,0},{2,1},{3,2},{4,3},{5,4},{6,5},{7,6},{8,7},{9,8},{10,9... | collective-permute-start | bytes 1544 | tf_op jit(solution)/shard_map/ppermute | solution.py:61
  323.2 1.2 collective-permute-done.33
  324.5 4.4 %collective-permute-start.36 = (f32[128,1]{0,1:T(1,128)S(1)}, f32[128,1]{0,1:T(1,128)S(1)}, u32[]{:S(2)}, u32[]{:S(2)}) collective-permute-start(f32[128,1]{0,1:T(1,128)S(1)} %collective-permute-done.34), channel_id=1, source_target_pairs={{0,15},{1,0},{2,1},{3,2},{4,3},{5,4},{6,5},{7,6},{8,7},{9,8},{10,9... | collective-permute-start | bytes 1544 | tf_op jit(solution)/shard_map/ppermute | solution.py:61
  330.2 4.4 %collective-permute-start.38 = (f32[128,1]{0,1:T(1,128)S(1)}, f32[128,1]{0,1:T(1,128)S(1)}, u32[]{:S(2)}, u32[]{:S(2)}) collective-permute-start(f32[128,1]{0,1:T(1,128)S(1)} %collective-permute-done.36), channel_id=1, source_target_pairs={{0,15},{1,0},{2,1},{3,2},{4,3},{5,4},{6,5},{7,6},{8,7},{9,8},{10,9... | collective-permute-start | bytes 1544 | tf_op jit(solution)/shard_map/ppermute | solution.py:61
  336.7 4.5 %collective-permute-start.40 = (f32[128,1]{0,1:T(1,128)S(1)}, f32[128,1]{0,1:T(1,128)S(1)}, u32[]{:S(2)}, u32[]{:S(2)}) collective-permute-start(f32[128,1]{0,1:T(1,128)S(1)} %collective-permute-done.38), channel_id=1, source_target_pairs={{0,15},{1,0},{2,1},{3,2},{4,3},{5,4},{6,5},{7,6},{8,7},{9,8},{10,9... | collective-permute-start | bytes 1544 | tf_op jit(solution)/shard_map/ppermute | solution.py:61
  342.5 4.7 %collective-permute-done.41 = f32[128,1]{0,1:T(1,128)S(1)} collective-permute-done((f32[128,1]{0,1:T(1,128)S(1)}, f32[128,1]{0,1:T(1,128)S(1)}, u32[]{:S(2)}, u32[]{:S(2)}) %collective-permute-start.41) | collective-permute-done | bytes 544 | tf_op jit(solution)/shard_map/ppermute | solution.py:58
  347.2 4.7 %fusion.42 = (bf16[128,2048]{1,0:T(8,128)(2,1)S(1)}, f32[128,2048]{1,0:T(8,128)S(1)}) fusion(bf16[2048,2048]{1,0:T(8,128)(2,1)} %param.13, bf16[128,128]{1,0:T(8,128)(2,1)S(1)} %collective-permute-done.24, bf16[128,1792]{1,0:T(8,128)(2,1)S(1)} %convert_element_type.25, bf16[128,128]{1,0:T(8,128)(2,1)S(1)} %collective-permute-done.23), kind=kOutput, calls=%fused_computation.88 | convolution fusion | flops 1075576832 | bytes 10485760 | tf_op jit(solution)/shard_map/dot_general | solution.py:48
  352.0 1.3 collective-permute-start.26
  353.3 3.0 collective-permute-start.25
  357.4 1.3 collective-permute-start.43
  358.7 3.3 collective-permute-start.42
  362.6 12.7 %fusion.43 = (bf16[128,2048]{1,0:T(8,128)(2,1)S(1)}, f32[128,2048]{1,0:T(8,128)S(1)}) fusion(f32[2048,2048]{1,0:T(8,128)} %reshape.335, f32[128,128]{1,0:T(8,128)S(1)} %collective-permute-done.43, f32[128,1792]{1,0:T(8,128)S(1)} %maximum_add_fusion.2, f32[128,128]{1,0:T(8,128)S(1)} %collective-permute-done.42), kind=kOutput, calls=%fused_computation.89 | convolution fusion | flops 6443237376 | bytes 19398656 | tf_op jit(solution)/shard_map/dot_general | solution.py:42
  375.4 1.3 collective-permute-start.45
  376.7 4.9 %collective-permute-start.44 = (bf16[128,128]{1,0:T(8,128)(2,1)S(1)}, bf16[128,128]{1,0:T(8,128)(2,1)S(1)}, u32[]{:S(2)}, u32[]{:S(2)}) collective-permute-start(bf16[128,128]{1,0:T(8,128)(2,1)S(1)} %get-tuple-element.30), channel_id=1, source_target_pairs={{0,1},{1,2},{2,3},{3,4},{4,5},{5,6},{6,7},{7,8},{8,9},{9,10},{10,1... | collective-permute-start | bytes 98312 | tf_op jit(solution)/shard_map/ppermute | solution.py:16
  383.1 32.5 %all-reduce = (f32[128]{0:T(128)}, f32[128]{0:T(128)}) all-reduce(f32[128]{0:T(128)S(1)} %get-tuple-element.3, f32[128]{0:T(128)S(1)} %get-tuple-element.2), channel_id=1, replica_groups=mesh['grp'=2,'tile'=16] {'tile'}, use_global_device_ids=true, to_apply=%region_8.9 | all-reduce | flops 256 | bytes 2048 | tf_op jit(solution)/shard_map/psum | solution.py:77
  416.3 3.1 multiply_subtract_fusion
  (153 shorter events, 22.2 us)
Async XLA Ops:
  0.6 64.4 %copy-start.7 = (f32[1792]{0:T(1024)S(1)}, f32[1792]{0:T(1024)}, u32[]{:S(2)}) copy-start(f32[1792]{0:T(1024)} %param.14) | copy-start | bytes 21508
  0.7 68.9 %copy-start.10 = (f32[7168]{0:T(1024)S(1)}, f32[7168]{0:T(1024)}, u32[]{:S(2)}) copy-start(f32[7168]{0:T(1024)} %param.12) | copy-start | bytes 86020
  2.3 12.8 %collective-permute-start.4 = (f32[128,1]{0,1:T(1,128)S(1)}, f32[128,1]{0,1:T(1,128)S(1)}, u32[]{:S(2)}, u32[]{:S(2)}) collective-permute-start(f32[128,1]{0,1:T(1,128)S(1)} %bitcast.21), channel_id=1, source_target_pairs={{0,1},{1,2},{2,3},{3,4},{4,5},{5,6},{6,7},{7,8},{8,9},{9,10},{10,1... | collective-permute-start | bytes 1544 | tf_op jit(solution)/shard_map/ppermute | solution.py:58
  2.9 12.4 %collective-permute-start.5 = (f32[128,1]{0,1:T(1,128)S(1)}, f32[128,1]{0,1:T(1,128)S(1)}, u32[]{:S(2)}, u32[]{:S(2)}) collective-permute-start(f32[128,1]{0,1:T(1,128)S(1)} %bitcast.22), channel_id=1, source_target_pairs={{0,15},{1,0},{2,1},{3,2},{4,3},{5,4},{6,5},{7,6},{8,7},{9,8},{10,9... | collective-permute-start | bytes 1544 | tf_op jit(solution)/shard_map/ppermute | solution.py:61
  7.9 47.2 %collective-permute-start.1 = (bf16[128,128]{1,0:T(8,128)(2,1)S(1)}, bf16[128,128]{1,0:T(8,128)(2,1)S(1)}, u32[]{:S(2)}, u32[]{:S(2)}) collective-permute-start(bf16[128,128]{1,0:T(8,128)(2,1)S(1)} %get-tuple-element.41), channel_id=1, source_target_pairs={{1,0},{2,1},{3,2},{4,3},{5,4},{6,5},{7,6},{8,7},{9,8},{10,9},{11,1... | collective-permute-start | bytes 98312 | tf_op jit(solution)/shard_map/ppermute | solution.py:19
  9.2 45.9 %collective-permute-start = (bf16[128,128]{1,0:T(8,128)(2,1)S(1)}, bf16[128,128]{1,0:T(8,128)(2,1)S(1)}, u32[]{:S(2)}, u32[]{:S(2)}) collective-permute-start(bf16[128,128]{1,0:T(8,128)(2,1)S(1)} %get-tuple-element.40), channel_id=1, source_target_pairs={{0,1},{1,2},{2,3},{3,4},{4,5},{5,6},{6,7},{7,8},{8,9},{9,10},{10,1... | collective-permute-start | bytes 98312 | tf_op jit(solution)/shard_map/ppermute | solution.py:16
  15.2 5.7 %collective-permute-start.6 = (f32[128,1]{0,1:T(1,128)S(1)}, f32[128,1]{0,1:T(1,128)S(1)}, u32[]{:S(2)}, u32[]{:S(2)}) collective-permute-start(f32[128,1]{0,1:T(1,128)S(1)} %collective-permute-done.4), channel_id=1, source_target_pairs={{0,1},{1,2},{2,3},{3,4},{4,5},{5,6},{6,7},{7,8},{8,9},{9,10},{10,1... | collective-permute-start | bytes 1544 | tf_op jit(solution)/shard_map/ppermute | solution.py:58
  15.3 5.7 %collective-permute-start.7 = (f32[128,1]{0,1:T(1,128)S(1)}, f32[128,1]{0,1:T(1,128)S(1)}, u32[]{:S(2)}, u32[]{:S(2)}) collective-permute-start(f32[128,1]{0,1:T(1,128)S(1)} %collective-permute-done.5), channel_id=1, source_target_pairs={{0,15},{1,0},{2,1},{3,2},{4,3},{5,4},{6,5},{7,6},{8,7},{9,8},{10,9... | collective-permute-start | bytes 1544 | tf_op jit(solution)/shard_map/ppermute | solution.py:61
  20.9 5.7 %collective-permute-start.8 = (f32[128,1]{0,1:T(1,128)S(1)}, f32[128,1]{0,1:T(1,128)S(1)}, u32[]{:S(2)}, u32[]{:S(2)}) collective-permute-start(f32[128,1]{0,1:T(1,128)S(1)} %collective-permute-done.6), channel_id=1, source_target_pairs={{0,1},{1,2},{2,3},{3,4},{4,5},{5,6},{6,7},{7,8},{8,9},{9,10},{10,1... | collective-permute-start | bytes 1544 | tf_op jit(solution)/shard_map/ppermute | solution.py:58
  21.0 6.4 %collective-permute-start.9 = (f32[128,1]{0,1:T(1,128)S(1)}, f32[128,1]{0,1:T(1,128)S(1)}, u32[]{:S(2)}, u32[]{:S(2)}) collective-permute-start(f32[128,1]{0,1:T(1,128)S(1)} %collective-permute-done.7), channel_id=1, source_target_pairs={{0,15},{1,0},{2,1},{3,2},{4,3},{5,4},{6,5},{7,6},{8,7},{9,8},{10,9... | collective-permute-start | bytes 1544 | tf_op jit(solution)/shard_map/ppermute | solution.py:61
  26.6 5.7 %collective-permute-start.10 = (f32[128,1]{0,1:T(1,128)S(1)}, f32[128,1]{0,1:T(1,128)S(1)}, u32[]{:S(2)}, u32[]{:S(2)}) collective-permute-start(f32[128,1]{0,1:T(1,128)S(1)} %collective-permute-done.8), channel_id=1, source_target_pairs={{0,1},{1,2},{2,3},{3,4},{4,5},{5,6},{6,7},{7,8},{8,9},{9,10},{10,1... | collective-permute-start | bytes 1544 | tf_op jit(solution)/shard_map/ppermute | solution.py:58
  27.4 5.7 %collective-permute-start.11 = (f32[128,1]{0,1:T(1,128)S(1)}, f32[128,1]{0,1:T(1,128)S(1)}, u32[]{:S(2)}, u32[]{:S(2)}) collective-permute-start(f32[128,1]{0,1:T(1,128)S(1)} %collective-permute-done.9), channel_id=1, source_target_pairs={{0,15},{1,0},{2,1},{3,2},{4,3},{5,4},{6,5},{7,6},{8,7},{9,8},{10,9... | collective-permute-start | bytes 1544 | tf_op jit(solution)/shard_map/ppermute | solution.py:61
  32.3 5.7 %collective-permute-start.12 = (f32[128,1]{0,1:T(1,128)S(1)}, f32[128,1]{0,1:T(1,128)S(1)}, u32[]{:S(2)}, u32[]{:S(2)}) collective-permute-start(f32[128,1]{0,1:T(1,128)S(1)} %collective-permute-done.10), channel_id=1, source_target_pairs={{0,1},{1,2},{2,3},{3,4},{4,5},{5,6},{6,7},{7,8},{8,9},{9,10},{10,1... | collective-permute-start | bytes 1544 | tf_op jit(solution)/shard_map/ppermute | solution.py:58
  33.1 5.7 %collective-permute-start.13 = (f32[128,1]{0,1:T(1,128)S(1)}, f32[128,1]{0,1:T(1,128)S(1)}, u32[]{:S(2)}, u32[]{:S(2)}) collective-permute-start(f32[128,1]{0,1:T(1,128)S(1)} %collective-permute-done.11), channel_id=1, source_target_pairs={{0,15},{1,0},{2,1},{3,2},{4,3},{5,4},{6,5},{7,6},{8,7},{9,8},{10,9... | collective-permute-start | bytes 1544 | tf_op jit(solution)/shard_map/ppermute | solution.py:61
  38.0 5.7 %collective-permute-start.14 = (f32[128,1]{0,1:T(1,128)S(1)}, f32[128,1]{0,1:T(1,128)S(1)}, u32[]{:S(2)}, u32[]{:S(2)}) collective-permute-start(f32[128,1]{0,1:T(1,128)S(1)} %collective-permute-done.12), channel_id=1, source_target_pairs={{0,1},{1,2},{2,3},{3,4},{4,5},{5,6},{6,7},{7,8},{8,9},{9,10},{10,1... | collective-permute-start | bytes 1544 | tf_op jit(solution)/shard_map/ppermute | solution.py:58
  38.8 5.7 %collective-permute-start.15 = (f32[128,1]{0,1:T(1,128)S(1)}, f32[128,1]{0,1:T(1,128)S(1)}, u32[]{:S(2)}, u32[]{:S(2)}) collective-permute-start(f32[128,1]{0,1:T(1,128)S(1)} %collective-permute-done.13), channel_id=1, source_target_pairs={{0,15},{1,0},{2,1},{3,2},{4,3},{5,4},{6,5},{7,6},{8,7},{9,8},{10,9... | collective-permute-start | bytes 1544 | tf_op jit(solution)/shard_map/ppermute | solution.py:61
  43.7 5.7 %collective-permute-start.16 = (f32[128,1]{0,1:T(1,128)S(1)}, f32[128,1]{0,1:T(1,128)S(1)}, u32[]{:S(2)}, u32[]{:S(2)}) collective-permute-start(f32[128,1]{0,1:T(1,128)S(1)} %collective-permute-done.14), channel_id=1, source_target_pairs={{0,1},{1,2},{2,3},{3,4},{4,5},{5,6},{6,7},{7,8},{8,9},{9,10},{10,1... | collective-permute-start | bytes 1544 | tf_op jit(solution)/shard_map/ppermute | solution.py:58
  44.5 5.7 %collective-permute-start.17 = (f32[128,1]{0,1:T(1,128)S(1)}, f32[128,1]{0,1:T(1,128)S(1)}, u32[]{:S(2)}, u32[]{:S(2)}) collective-permute-start(f32[128,1]{0,1:T(1,128)S(1)} %collective-permute-done.15), channel_id=1, source_target_pairs={{0,15},{1,0},{2,1},{3,2},{4,3},{5,4},{6,5},{7,6},{8,7},{9,8},{10,9... | collective-permute-start | bytes 1544 | tf_op jit(solution)/shard_map/ppermute | solution.py:61
  49.4 5.7 %collective-permute-start.18 = (f32[128,1]{0,1:T(1,128)S(1)}, f32[128,1]{0,1:T(1,128)S(1)}, u32[]{:S(2)}, u32[]{:S(2)}) collective-permute-start(f32[128,1]{0,1:T(1,128)S(1)} %collective-permute-done.16), channel_id=1, source_target_pairs={{0,1},{1,2},{2,3},{3,4},{4,5},{5,6},{6,7},{7,8},{8,9},{9,10},{10,1... | collective-permute-start | bytes 1544 | tf_op jit(solution)/shard_map/ppermute | solution.py:58
  59.9 4.5 %collective-permute-start.3 = (bf16[128,128]{1,0:T(8,128)(2,1)S(1)}, bf16[128,128]{1,0:T(8,128)(2,1)S(1)}, u32[]{:S(2)}, u32[]{:S(2)}) collective-permute-start(bf16[128,128]{1,0:T(8,128)(2,1)S(1)} %get-tuple-element.37), channel_id=1, source_target_pairs={{1,0},{2,1},{3,2},{4,3},{5,4},{6,5},{7,6},{8,7},{9,8},{10,9},{11,1... | collective-permute-start | bytes 98312 | tf_op jit(solution)/shard_map/ppermute | solution.py:19
  61.2 3.9 collective-permute-start.2
  65.2 178.9 %collective-permute-start.20 = (f32[128,128]{1,0:T(8,128)S(1)}, f32[128,128]{1,0:T(8,128)S(1)}, u32[]{:S(2)}, u32[]{:S(2)}) collective-permute-start(f32[128,128]{1,0:T(8,128)S(1)} %get-tuple-element.27), channel_id=1, source_target_pairs={{1,0},{2,1},{3,2},{4,3},{5,4},{6,5},{7,6},{8,7},{9,8},{10,9},{11,1... | collective-permute-start | bytes 196616 | tf_op jit(solution)/shard_map/ppermute | solution.py:19
  66.5 177.6 %collective-permute-start.19 = (f32[128,128]{1,0:T(8,128)S(1)}, f32[128,128]{1,0:T(8,128)S(1)}, u32[]{:S(2)}, u32[]{:S(2)}) collective-permute-start(f32[128,128]{1,0:T(8,128)S(1)} %get-tuple-element.26), channel_id=1, source_target_pairs={{0,1},{1,2},{2,3},{3,4},{4,5},{5,6},{6,7},{7,8},{8,9},{9,10},{10,1... | collective-permute-start | bytes 196616 | tf_op jit(solution)/shard_map/ppermute | solution.py:16
  257.0 5.9 %collective-permute-start.22 = (bf16[128,128]{1,0:T(8,128)(2,1)S(1)}, bf16[128,128]{1,0:T(8,128)(2,1)S(1)}, u32[]{:S(2)}, u32[]{:S(2)}) collective-permute-start(bf16[128,128]{1,0:T(8,128)(2,1)S(1)} %get-tuple-element.35), channel_id=1, source_target_pairs={{1,0},{2,1},{3,2},{4,3},{5,4},{6,5},{7,6},{8,7},{9,8},{10,9},{11,1... | collective-permute-start | bytes 98312 | tf_op jit(solution)/shard_map/ppermute | solution.py:19
  258.3 5.4 %collective-permute-start.21 = (bf16[128,128]{1,0:T(8,128)(2,1)S(1)}, bf16[128,128]{1,0:T(8,128)(2,1)S(1)}, u32[]{:S(2)}, u32[]{:S(2)}) collective-permute-start(bf16[128,128]{1,0:T(8,128)(2,1)S(1)} %get-tuple-element.34), channel_id=1, source_target_pairs={{0,1},{1,2},{2,3},{3,4},{4,5},{5,6},{6,7},{7,8},{8,9},{9,10},{10,1... | collective-permute-start | bytes 98312 | tf_op jit(solution)/shard_map/ppermute | solution.py:16
  297.3 50.0 %collective-permute-start.24 = (bf16[128,128]{1,0:T(8,128)(2,1)S(1)}, bf16[128,128]{1,0:T(8,128)(2,1)S(1)}, u32[]{:S(2)}, u32[]{:S(2)}) collective-permute-start(bf16[128,128]{1,0:T(8,128)(2,1)S(1)} %get-tuple-element.39), channel_id=1, source_target_pairs={{1,0},{2,1},{3,2},{4,3},{5,4},{6,5},{7,6},{8,7},{9,8},{10,9},{11,1... | collective-permute-start | bytes 98312 | tf_op jit(solution)/shard_map/ppermute | solution.py:19
  298.6 48.7 %collective-permute-start.23 = (bf16[128,128]{1,0:T(8,128)(2,1)S(1)}, bf16[128,128]{1,0:T(8,128)(2,1)S(1)}, u32[]{:S(2)}, u32[]{:S(2)}) collective-permute-start(bf16[128,128]{1,0:T(8,128)(2,1)S(1)} %get-tuple-element.38), channel_id=1, source_target_pairs={{0,1},{1,2},{2,3},{3,4},{4,5},{5,6},{6,7},{7,8},{8,9},{9,10},{10,1... | collective-permute-start | bytes 98312 | tf_op jit(solution)/shard_map/ppermute | solution.py:16
  301.6 5.7 %collective-permute-start.27 = (f32[128,1]{0,1:T(1,128)S(1)}, f32[128,1]{0,1:T(1,128)S(1)}, u32[]{:S(2)}, u32[]{:S(2)}) collective-permute-start(f32[128,1]{0,1:T(1,128)S(1)} %bitcast.24), channel_id=1, source_target_pairs={{0,1},{1,2},{2,3},{3,4},{4,5},{5,6},{6,7},{7,8},{8,9},{9,10},{10,1... | collective-permute-start | bytes 1544 | tf_op jit(solution)/shard_map/ppermute | solution.py:58
  301.7 5.7 %collective-permute-start.28 = (f32[128,1]{0,1:T(1,128)S(1)}, f32[128,1]{0,1:T(1,128)S(1)}, u32[]{:S(2)}, u32[]{:S(2)}) collective-permute-start(f32[128,1]{0,1:T(1,128)S(1)} %bitcast.25), channel_id=1, source_target_pairs={{0,15},{1,0},{2,1},{3,2},{4,3},{5,4},{6,5},{7,6},{8,7},{9,8},{10,9... | collective-permute-start | bytes 1544 | tf_op jit(solution)/shard_map/ppermute | solution.py:61
  307.3 5.7 %collective-permute-start.29 = (f32[128,1]{0,1:T(1,128)S(1)}, f32[128,1]{0,1:T(1,128)S(1)}, u32[]{:S(2)}, u32[]{:S(2)}) collective-permute-start(f32[128,1]{0,1:T(1,128)S(1)} %collective-permute-done.27), channel_id=1, source_target_pairs={{0,1},{1,2},{2,3},{3,4},{4,5},{5,6},{6,7},{7,8},{8,9},{9,10},{10,1... | collective-permute-start | bytes 1544 | tf_op jit(solution)/shard_map/ppermute | solution.py:58
  307.4 5.7 %collective-permute-start.30 = (f32[128,1]{0,1:T(1,128)S(1)}, f32[128,1]{0,1:T(1,128)S(1)}, u32[]{:S(2)}, u32[]{:S(2)}) collective-permute-start(f32[128,1]{0,1:T(1,128)S(1)} %collective-permute-done.28), channel_id=1, source_target_pairs={{0,15},{1,0},{2,1},{3,2},{4,3},{5,4},{6,5},{7,6},{8,7},{9,8},{10,9... | collective-permute-start | bytes 1544 | tf_op jit(solution)/shard_map/ppermute | solution.py:61
  313.0 5.7 %collective-permute-start.31 = (f32[128,1]{0,1:T(1,128)S(1)}, f32[128,1]{0,1:T(1,128)S(1)}, u32[]{:S(2)}, u32[]{:S(2)}) collective-permute-start(f32[128,1]{0,1:T(1,128)S(1)} %collective-permute-done.29), channel_id=1, source_target_pairs={{0,1},{1,2},{2,3},{3,4},{4,5},{5,6},{6,7},{7,8},{8,9},{9,10},{10,1... | collective-permute-start | bytes 1544 | tf_op jit(solution)/shard_map/ppermute | solution.py:58
  313.1 5.7 %collective-permute-start.32 = (f32[128,1]{0,1:T(1,128)S(1)}, f32[128,1]{0,1:T(1,128)S(1)}, u32[]{:S(2)}, u32[]{:S(2)}) collective-permute-start(f32[128,1]{0,1:T(1,128)S(1)} %collective-permute-done.30), channel_id=1, source_target_pairs={{0,15},{1,0},{2,1},{3,2},{4,3},{5,4},{6,5},{7,6},{8,7},{9,8},{10,9... | collective-permute-start | bytes 1544 | tf_op jit(solution)/shard_map/ppermute | solution.py:61
  318.7 5.7 %collective-permute-start.33 = (f32[128,1]{0,1:T(1,128)S(1)}, f32[128,1]{0,1:T(1,128)S(1)}, u32[]{:S(2)}, u32[]{:S(2)}) collective-permute-start(f32[128,1]{0,1:T(1,128)S(1)} %collective-permute-done.31), channel_id=1, source_target_pairs={{0,1},{1,2},{2,3},{3,4},{4,5},{5,6},{6,7},{7,8},{8,9},{9,10},{10,1... | collective-permute-start | bytes 1544 | tf_op jit(solution)/shard_map/ppermute | solution.py:58
  318.8 5.7 %collective-permute-start.34 = (f32[128,1]{0,1:T(1,128)S(1)}, f32[128,1]{0,1:T(1,128)S(1)}, u32[]{:S(2)}, u32[]{:S(2)}) collective-permute-start(f32[128,1]{0,1:T(1,128)S(1)} %collective-permute-done.32), channel_id=1, source_target_pairs={{0,15},{1,0},{2,1},{3,2},{4,3},{5,4},{6,5},{7,6},{8,7},{9,8},{10,9... | collective-permute-start | bytes 1544 | tf_op jit(solution)/shard_map/ppermute | solution.py:61
  324.4 5.7 %collective-permute-start.35 = (f32[128,1]{0,1:T(1,128)S(1)}, f32[128,1]{0,1:T(1,128)S(1)}, u32[]{:S(2)}, u32[]{:S(2)}) collective-permute-start(f32[128,1]{0,1:T(1,128)S(1)} %collective-permute-done.33), channel_id=1, source_target_pairs={{0,1},{1,2},{2,3},{3,4},{4,5},{5,6},{6,7},{7,8},{8,9},{9,10},{10,1... | collective-permute-start | bytes 1544 | tf_op jit(solution)/shard_map/ppermute | solution.py:58
  324.5 5.7 %collective-permute-start.36 = (f32[128,1]{0,1:T(1,128)S(1)}, f32[128,1]{0,1:T(1,128)S(1)}, u32[]{:S(2)}, u32[]{:S(2)}) collective-permute-start(f32[128,1]{0,1:T(1,128)S(1)} %collective-permute-done.34), channel_id=1, source_target_pairs={{0,15},{1,0},{2,1},{3,2},{4,3},{5,4},{6,5},{7,6},{8,7},{9,8},{10,9... | collective-permute-start | bytes 1544 | tf_op jit(solution)/shard_map/ppermute | solution.py:61
  330.1 5.7 %collective-permute-start.37 = (f32[128,1]{0,1:T(1,128)S(1)}, f32[128,1]{0,1:T(1,128)S(1)}, u32[]{:S(2)}, u32[]{:S(2)}) collective-permute-start(f32[128,1]{0,1:T(1,128)S(1)} %collective-permute-done.35), channel_id=1, source_target_pairs={{0,1},{1,2},{2,3},{3,4},{4,5},{5,6},{6,7},{7,8},{8,9},{9,10},{10,1... | collective-permute-start | bytes 1544 | tf_op jit(solution)/shard_map/ppermute | solution.py:58
  330.2 6.5 %collective-permute-start.38 = (f32[128,1]{0,1:T(1,128)S(1)}, f32[128,1]{0,1:T(1,128)S(1)}, u32[]{:S(2)}, u32[]{:S(2)}) collective-permute-start(f32[128,1]{0,1:T(1,128)S(1)} %collective-permute-done.36), channel_id=1, source_target_pairs={{0,15},{1,0},{2,1},{3,2},{4,3},{5,4},{6,5},{7,6},{8,7},{9,8},{10,9... | collective-permute-start | bytes 1544 | tf_op jit(solution)/shard_map/ppermute | solution.py:61
  335.8 5.7 %collective-permute-start.39 = (f32[128,1]{0,1:T(1,128)S(1)}, f32[128,1]{0,1:T(1,128)S(1)}, u32[]{:S(2)}, u32[]{:S(2)}) collective-permute-start(f32[128,1]{0,1:T(1,128)S(1)} %collective-permute-done.37), channel_id=1, source_target_pairs={{0,1},{1,2},{2,3},{3,4},{4,5},{5,6},{6,7},{7,8},{8,9},{9,10},{10,1... | collective-permute-start | bytes 1544 | tf_op jit(solution)/shard_map/ppermute | solution.py:58
  336.7 5.8 %collective-permute-start.40 = (f32[128,1]{0,1:T(1,128)S(1)}, f32[128,1]{0,1:T(1,128)S(1)}, u32[]{:S(2)}, u32[]{:S(2)}) collective-permute-start(f32[128,1]{0,1:T(1,128)S(1)} %collective-permute-done.38), channel_id=1, source_target_pairs={{0,15},{1,0},{2,1},{3,2},{4,3},{5,4},{6,5},{7,6},{8,7},{9,8},{10,9... | collective-permute-start | bytes 1544 | tf_op jit(solution)/shard_map/ppermute | solution.py:61
  341.5 5.7 %collective-permute-start.41 = (f32[128,1]{0,1:T(1,128)S(1)}, f32[128,1]{0,1:T(1,128)S(1)}, u32[]{:S(2)}, u32[]{:S(2)}) collective-permute-start(f32[128,1]{0,1:T(1,128)S(1)} %collective-permute-done.39), channel_id=1, source_target_pairs={{0,1},{1,2},{2,3},{3,4},{4,5},{5,6},{6,7},{7,8},{8,9},{9,10},{10,1... | collective-permute-start | bytes 1544 | tf_op jit(solution)/shard_map/ppermute | solution.py:58
  352.0 5.2 %collective-permute-start.26 = (bf16[128,128]{1,0:T(8,128)(2,1)S(1)}, bf16[128,128]{1,0:T(8,128)(2,1)S(1)}, u32[]{:S(2)}, u32[]{:S(2)}) collective-permute-start(bf16[128,128]{1,0:T(8,128)(2,1)S(1)} %get-tuple-element.33), channel_id=1, source_target_pairs={{1,0},{2,1},{3,2},{4,3},{5,4},{6,5},{7,6},{8,7},{9,8},{10,9},{11,1... | collective-permute-start | bytes 98312 | tf_op jit(solution)/shard_map/ppermute | solution.py:19
  353.3 3.9 collective-permute-start.25
  357.4 4.6 %collective-permute-start.43 = (f32[128,128]{1,0:T(8,128)S(1)}, f32[128,128]{1,0:T(8,128)S(1)}, u32[]{:S(2)}, u32[]{:S(2)}) collective-permute-start(f32[128,128]{1,0:T(8,128)S(1)} %get-tuple-element.25), channel_id=1, source_target_pairs={{1,0},{2,1},{3,2},{4,3},{5,4},{6,5},{7,6},{8,7},{9,8},{10,9},{11,1... | collective-permute-start | bytes 196616 | tf_op jit(solution)/shard_map/ppermute | solution.py:19
  358.7 3.9 collective-permute-start.42
  375.4 6.3 %collective-permute-start.45 = (bf16[128,128]{1,0:T(8,128)(2,1)S(1)}, bf16[128,128]{1,0:T(8,128)(2,1)S(1)}, u32[]{:S(2)}, u32[]{:S(2)}) collective-permute-start(bf16[128,128]{1,0:T(8,128)(2,1)S(1)} %get-tuple-element.31), channel_id=1, source_target_pairs={{1,0},{2,1},{3,2},{4,3},{5,4},{6,5},{7,6},{8,7},{9,8},{10,9},{11,1... | collective-permute-start | bytes 98312 | tf_op jit(solution)/shard_map/ppermute | solution.py:19
  376.7 5.8 %collective-permute-start.44 = (bf16[128,128]{1,0:T(8,128)(2,1)S(1)}, bf16[128,128]{1,0:T(8,128)(2,1)S(1)}, u32[]{:S(2)}, u32[]{:S(2)}) collective-permute-start(bf16[128,128]{1,0:T(8,128)(2,1)S(1)} %get-tuple-element.30), channel_id=1, source_target_pairs={{0,1},{1,2},{2,3},{3,4},{4,5},{5,6},{6,7},{7,8},{8,9},{9,10},{10,1... | collective-permute-start | bytes 98312 | tf_op jit(solution)/shard_map/ppermute | solution.py:16
  (14 other events, 280.7 us)
